TPU v7x, 512 devices: a whole 4x4x16 slice. The times are simulated.
512 devices in a mesh: guide: 2 (over core), patch: 256 (over x, y, z).
Axes of the slice: x: 4, y: 4, z: 16, core: 2. Of those that a mesh axis runs over, the one named last changes fastest.
Arguments:
- queries: bfloat16 [2, 28672, 128], P('guide', 'patch'), may hold values from -40 to 40
- fresh_keys: bfloat16 [2, 28672, 128], P('guide', 'patch'), may hold values from -9.5625 to 9.5625
- fresh_values: bfloat16 [2, 28672, 128], P('guide', 'patch'), may hold values from -6 to 6
- stale_keys: bfloat16 [2, 28672, 128], P('guide', 'patch'), may hold values from -10 to 10
- stale_values: bfloat16 [2, 28672, 128], P('guide', 'patch'), may hold values from -6 to 6
- hidden: bfloat16 [2, 28672, 5120], P('guide', 'patch'), may hold values from -6 to 6
- out_weight: bfloat16 [128, 5120], replicated, may hold values from -0.5 to 0.5
- modulation: float32 [5120], replicated, may hold values from 1 to 4
Outputs:
- guided: bfloat16 [28672, 5120], P('patch', 'guide')
All inputs are finite; a program needn't handle non-finite values.
Results may differ from a plain program's by a relative error of at most 0.0051.
Values may be sent and summed in bfloat16 or wider, within the bound.
No kernel may reach another device: no remote copies, remote signals or barrier semaphores. Data moves between devices by JAX's collectives and lax.ppermute only.
A program may use at most 64 MiB of HBM per device.

v0:
```python
import math
import jax
import jax.numpy as jnp
from jax import lax
from jax.sharding import PartitionSpec as P

GUIDANCE = 5.0


def swapped(value, axis, stride):
    mask = 2**stride
    pairs = [(source, source ^ mask) for source in range(lax.axis_size(axis))]
    return lax.ppermute(value, axis, pairs)


def block_length(local_rows, patches):
    shards = 1
    while shards * 2 * local_rows <= 4096 and patches % (shards * 2) == 0:
        shards = shards * 2
    return shards * local_rows


def on_device(
    queries, fresh_keys, fresh_values, stale_keys, stale_values, hidden, out_weight, modulation
):
    query_rows = queries[0]
    keys_fresh = fresh_keys[0]
    values_fresh = fresh_values[0]
    local_rows = query_rows.shape[0]
    head_width = query_rows.shape[1]
    patches = lax.axis_size("patch")
    own_start = lax.axis_index("patch") * local_rows
    score_scale = 1.0 / math.sqrt(head_width)
    block_size = block_length(local_rows, patches)

    def refresh(piece_keys, piece_values, first_row):
        piece_rows = piece_keys.shape[0]
        position = first_row + jnp.arange(piece_rows, dtype=jnp.int32)
        inside = (position >= own_start) & (position < own_start + local_rows)
        offset = jnp.clip(position - own_start, 0, local_rows - 1)
        new_keys = jnp.where(inside[:, None], jnp.take(keys_fresh, offset, axis=0), piece_keys)
        new_values = jnp.where(
            inside[:, None], jnp.take(values_fresh, offset, axis=0), piece_values
        )
        return (new_keys, new_values)

    def attend_block(running, piece_keys, piece_values, first_row):
        running_max, running_sum, running_acc = running
        piece_keys, piece_values = refresh(piece_keys, piece_values, first_row)
        scores = (
            lax.dot_general(
                query_rows, piece_keys, (((1,), (1,)), ((), ())), preferred_element_type=jnp.float32
            )
            * score_scale
        )
        new_max = jnp.maximum(running_max, jnp.max(scores, axis=1))
        factor = jnp.exp(running_max - new_max)
        weights = jnp.exp(scores - new_max[:, None]).astype(jnp.bfloat16)
        new_sum = running_sum * factor + jnp.sum(weights.astype(jnp.float32), axis=1)
        new_acc = running_acc * factor[:, None] + jnp.dot(
            weights, piece_values, preferred_element_type=jnp.float32
        )
        return (new_max, new_sum, new_acc)

    initial = (
        jnp.full((local_rows,), -1e30, jnp.float32),
        jnp.zeros((local_rows,), jnp.float32),
        jnp.zeros((local_rows, head_width), jnp.float32),
    )
    all_keys, all_values = (
        lax.all_gather(stale_keys[0], "patch", axis=0, tiled=True),
        lax.all_gather(stale_values[0], "patch", axis=0, tiled=True),
    )
    running = initial
    piece_keys = all_keys
    piece_values = all_values
    piece_rows = piece_keys.shape[0]
    step_rows = math.gcd(piece_rows, block_size)
    step_count = piece_rows // step_rows
    grouped_keys = piece_keys.reshape(step_count, step_rows, head_width)
    grouped_values = piece_values.reshape(step_count, step_rows, head_width)

    def advance(current, element):
        number, block_keys, block_values = element
        return (attend_block(current, block_keys, block_values, number * step_rows), None)

    running, unused = lax.scan(
        advance, running, (jnp.arange(step_count, dtype=jnp.int32), grouped_keys, grouped_values)
    )
    attention = (running[2] / running[1][:, None]).astype(jnp.bfloat16)
    projected = jnp.dot(attention, out_weight, preferred_element_type=jnp.float32)
    branch_out = (hidden[0].astype(jnp.float32) + modulation[None, :] * projected).astype(
        jnp.bfloat16
    )
    half_width = branch_out.shape[1] // 2
    side = lax.axis_index("guide")
    partner = swapped(branch_out, "guide", 0)
    conditional = jnp.where(side == 0, branch_out, partner)
    unconditional = jnp.where(side == 0, partner, branch_out)
    conditional = lax.dynamic_slice_in_dim(conditional, side * half_width, half_width, 1)
    unconditional = lax.dynamic_slice_in_dim(unconditional, side * half_width, half_width, 1)
    cond_value = conditional.astype(jnp.float32)
    uncond_value = unconditional.astype(jnp.float32)
    return (uncond_value + GUIDANCE * (cond_value - uncond_value)).astype(jnp.bfloat16)


def solution(mesh):
    in_specs = (
        P("guide", "patch", None),
        P("guide", "patch", None),
        P("guide", "patch", None),
        P("guide", "patch", None),
        P("guide", "patch", None),
        P("guide", "patch", None),
        P(),
        P(),
    )
    out_specs = P("patch", "guide")
    return jax.shard_map(
        on_device, mesh=mesh, in_specs=in_specs, out_specs=out_specs, check_vma=False
    )
```

profile of v0, /device:TPU:1, one launch (start us, length us, event | category | flops | bytes accessed | tf_op | source)
XLA Modules:
  0.0 678.7 jit_solution(15807300499211732269)
XLA Ops:
  6.5 0.7 all-gather.5.cloned.1.call-update
  7.3 0.7 all-gather.7.cloned.1.call-update
  8.0 217.2 %all-gather.5.cloned.1.call-done = bf16[1,28672,128]{2,1,0:T(8,128)(2,1)} async-done(((bf16[1,112,128]{2,1,0:T(8,128)(2,1)}), bf16[1,28672,128]{2,1,0:T(8,128)(2,1)}) %all-gather.5.cloned.1.call-update) | async-done | bytes 7340048 | tf_op jit(solution)/shard_map/all_gather | solution.py:71
  225.3 216.4 %all-gather.7.cloned.1.call-done = bf16[1,28672,128]{2,1,0:T(8,128)(2,1)} async-done(((bf16[1,112,128]{2,1,0:T(8,128)(2,1)}), bf16[1,28672,128]{2,1,0:T(8,128)(2,1)}) %all-gather.7.cloned.1.call-update) | async-done | bytes 7340048 | tf_op jit(solution)/shard_map/all_gather | solution.py:72
  441.6 212.1 %while.16 = (s32[]{:T(128)}, f32[112]{0:T(128)S(1)}, f32[112]{0:T(128)S(1)}, f32[112,128]{1,0:T(8,128)S(1)}, s32[8]{0:T(128)S(1)}, /*index=5*/s32[]{:T(128)}, s3...) while((s32[]{:T(128)}, f32[112]{0:T(128)S(1)}, ...), condition=%wide.region_3.5_spmd.clone, body=%wide.region_0.4_spmd.clone.sunk | while | flops 210679344 | bytes 12748057 | solution.py:87
  441.6 0.6 dynamic_slice.46
  442.9 8.1 %gather_fusion = bf16[3584,128]{1,0:T(8,128)(2,1)} fusion(bf16[112,128]{1,0:T(8,128)(2,1)S(1)} %copy-done.1, s32[4096]{0:T(1024)S(1)} %pad_clamp_fusion.2), kind=kCustom, calls=%fused_computation.clone.clone.1 | custom fusion | bytes 1849344 | tf_op jit(solution)/shard_map/while/body/eval_jaxpr/jit(_take)/gather | solution.py:41
  451.0 4.5 fusion.35
  455.5 0.4 convert_reduce_fusion.2
  455.9 0.3 copy-done.2
  456.2 8.1 %gather_fusion.1 = bf16[3584,128]{1,0:T(8,128)(2,1)} fusion(bf16[112,128]{1,0:T(8,128)(2,1)S(1)} %copy-done.2, s32[4096]{0:T(1024)S(1)} %pad_clamp_fusion.2), kind=kCustom, calls=%fused_computation.1.clone.clone.1 | custom fusion | bytes 1849344 | tf_op jit(solution)/shard_map/while/body/eval_jaxpr/jit(_take)/gather | solution.py:43
  464.4 3.8 convolution_add_fusion.2
  468.2 0.6 dynamic_slice.46
  469.4 8.1 %gather_fusion = bf16[3584,128]{1,0:T(8,128)(2,1)} fusion(bf16[112,128]{1,0:T(8,128)(2,1)S(1)} %copy-done.1, s32[4096]{0:T(1024)S(1)} %pad_clamp_fusion.2), kind=kCustom, calls=%fused_computation.clone.clone.1 | custom fusion | bytes 1849344 | tf_op jit(solution)/shard_map/while/body/eval_jaxpr/jit(_take)/gather | solution.py:41
  477.5 4.5 fusion.35
  482.0 0.4 convert_reduce_fusion.2
  482.4 0.3 copy-done.2
  482.7 8.1 %gather_fusion.1 = bf16[3584,128]{1,0:T(8,128)(2,1)} fusion(bf16[112,128]{1,0:T(8,128)(2,1)S(1)} %copy-done.2, s32[4096]{0:T(1024)S(1)} %pad_clamp_fusion.2), kind=kCustom, calls=%fused_computation.1.clone.clone.1 | custom fusion | bytes 1849344 | tf_op jit(solution)/shard_map/while/body/eval_jaxpr/jit(_take)/gather | solution.py:43
  490.9 3.8 convolution_add_fusion.2
  494.7 0.6 dynamic_slice.46
  495.9 8.1 %gather_fusion = bf16[3584,128]{1,0:T(8,128)(2,1)} fusion(bf16[112,128]{1,0:T(8,128)(2,1)S(1)} %copy-done.1, s32[4096]{0:T(1024)S(1)} %pad_clamp_fusion.2), kind=kCustom, calls=%fused_computation.clone.clone.1 | custom fusion | bytes 1849344 | tf_op jit(solution)/shard_map/while/body/eval_jaxpr/jit(_take)/gather | solution.py:41
  504.0 4.5 fusion.35
  508.5 0.4 convert_reduce_fusion.2
  508.9 0.3 copy-done.2
  509.3 8.1 %gather_fusion.1 = bf16[3584,128]{1,0:T(8,128)(2,1)} fusion(bf16[112,128]{1,0:T(8,128)(2,1)S(1)} %copy-done.2, s32[4096]{0:T(1024)S(1)} %pad_clamp_fusion.2), kind=kCustom, calls=%fused_computation.1.clone.clone.1 | custom fusion | bytes 1849344 | tf_op jit(solution)/shard_map/while/body/eval_jaxpr/jit(_take)/gather | solution.py:43
  517.4 3.8 convolution_add_fusion.2
  521.2 0.6 dynamic_slice.46
  522.4 8.1 %gather_fusion = bf16[3584,128]{1,0:T(8,128)(2,1)} fusion(bf16[112,128]{1,0:T(8,128)(2,1)S(1)} %copy-done.1, s32[4096]{0:T(1024)S(1)} %pad_clamp_fusion.2), kind=kCustom, calls=%fused_computation.clone.clone.1 | custom fusion | bytes 1849344 | tf_op jit(solution)/shard_map/while/body/eval_jaxpr/jit(_take)/gather | solution.py:41
  530.6 4.5 fusion.35
  535.0 0.4 convert_reduce_fusion.2
  535.4 0.3 copy-done.2
  535.8 8.1 %gather_fusion.1 = bf16[3584,128]{1,0:T(8,128)(2,1)} fusion(bf16[112,128]{1,0:T(8,128)(2,1)S(1)} %copy-done.2, s32[4096]{0:T(1024)S(1)} %pad_clamp_fusion.2), kind=kCustom, calls=%fused_computation.1.clone.clone.1 | custom fusion | bytes 1849344 | tf_op jit(solution)/shard_map/while/body/eval_jaxpr/jit(_take)/gather | solution.py:43
  543.9 3.8 convolution_add_fusion.2
  547.7 0.6 dynamic_slice.46
  548.9 8.1 %gather_fusion = bf16[3584,128]{1,0:T(8,128)(2,1)} fusion(bf16[112,128]{1,0:T(8,128)(2,1)S(1)} %copy-done.1, s32[4096]{0:T(1024)S(1)} %pad_clamp_fusion.2), kind=kCustom, calls=%fused_computation.clone.clone.1 | custom fusion | bytes 1849344 | tf_op jit(solution)/shard_map/while/body/eval_jaxpr/jit(_take)/gather | solution.py:41
  557.1 4.5 fusion.35
  561.6 0.4 convert_reduce_fusion.2
  562.0 0.3 copy-done.2
  562.3 8.1 %gather_fusion.1 = bf16[3584,128]{1,0:T(8,128)(2,1)} fusion(bf16[112,128]{1,0:T(8,128)(2,1)S(1)} %copy-done.2, s32[4096]{0:T(1024)S(1)} %pad_clamp_fusion.2), kind=kCustom, calls=%fused_computation.1.clone.clone.1 | custom fusion | bytes 1849344 | tf_op jit(solution)/shard_map/while/body/eval_jaxpr/jit(_take)/gather | solution.py:43
  570.4 3.8 convolution_add_fusion.2
  574.2 0.6 dynamic_slice.46
  575.5 8.1 %gather_fusion = bf16[3584,128]{1,0:T(8,128)(2,1)} fusion(bf16[112,128]{1,0:T(8,128)(2,1)S(1)} %copy-done.1, s32[4096]{0:T(1024)S(1)} %pad_clamp_fusion.2), kind=kCustom, calls=%fused_computation.clone.clone.1 | custom fusion | bytes 1849344 | tf_op jit(solution)/shard_map/while/body/eval_jaxpr/jit(_take)/gather | solution.py:41
  583.6 4.5 fusion.35
  588.1 0.4 convert_reduce_fusion.2
  588.5 0.3 copy-done.2
  588.8 8.1 %gather_fusion.1 = bf16[3584,128]{1,0:T(8,128)(2,1)} fusion(bf16[112,128]{1,0:T(8,128)(2,1)S(1)} %copy-done.2, s32[4096]{0:T(1024)S(1)} %pad_clamp_fusion.2), kind=kCustom, calls=%fused_computation.1.clone.clone.1 | custom fusion | bytes 1849344 | tf_op jit(solution)/shard_map/while/body/eval_jaxpr/jit(_take)/gather | solution.py:43
  596.9 3.8 convolution_add_fusion.2
  600.7 0.6 dynamic_slice.46
  602.0 8.1 %gather_fusion = bf16[3584,128]{1,0:T(8,128)(2,1)} fusion(bf16[112,128]{1,0:T(8,128)(2,1)S(1)} %copy-done.1, s32[4096]{0:T(1024)S(1)} %pad_clamp_fusion.2), kind=kCustom, calls=%fused_computation.clone.clone.1 | custom fusion | bytes 1849344 | tf_op jit(solution)/shard_map/while/body/eval_jaxpr/jit(_take)/gather | solution.py:41
  610.1 4.5 fusion.35
  614.6 0.4 convert_reduce_fusion.2
  615.0 0.3 copy-done.2
  615.3 8.1 %gather_fusion.1 = bf16[3584,128]{1,0:T(8,128)(2,1)} fusion(bf16[112,128]{1,0:T(8,128)(2,1)S(1)} %copy-done.2, s32[4096]{0:T(1024)S(1)} %pad_clamp_fusion.2), kind=kCustom, calls=%fused_computation.1.clone.clone.1 | custom fusion | bytes 1849344 | tf_op jit(solution)/shard_map/while/body/eval_jaxpr/jit(_take)/gather | solution.py:43
  623.5 3.8 convolution_add_fusion.2
  627.3 0.6 dynamic_slice.46
  628.5 8.1 %gather_fusion = bf16[3584,128]{1,0:T(8,128)(2,1)} fusion(bf16[112,128]{1,0:T(8,128)(2,1)S(1)} %copy-done.1, s32[4096]{0:T(1024)S(1)} %pad_clamp_fusion.2), kind=kCustom, calls=%fused_computation.clone.clone.1 | custom fusion | bytes 1849344 | tf_op jit(solution)/shard_map/while/body/eval_jaxpr/jit(_take)/gather | solution.py:41
  636.6 4.5 fusion.35
  641.1 0.4 convert_reduce_fusion.2
  641.8 8.1 %gather_fusion.1 = bf16[3584,128]{1,0:T(8,128)(2,1)} fusion(bf16[112,128]{1,0:T(8,128)(2,1)S(1)} %copy-done.2, s32[4096]{0:T(1024)S(1)} %pad_clamp_fusion.2), kind=kCustom, calls=%fused_computation.1.clone.clone.1 | custom fusion | bytes 1849344 | tf_op jit(solution)/shard_map/while/body/eval_jaxpr/jit(_take)/gather | solution.py:43
  650.0 3.8 convolution_add_fusion.2
  653.8 1.8 fusion.21
  655.6 11.6 %collective-permute-start = (bf16[112,5120]{1,0:T(8,128)(2,1)S(1)}, bf16[112,5120]{1,0:T(8,128)(2,1)}, u32[]{:S(2)}, u32[]{:S(2)}) collective-permute-start(bf16[112,5120]{1,0:T(8,128)(2,1)S(1)} %fusion.21), channel_id=1, source_target_pairs={{0,256},{256,0},{1,257},{257,1},{2,258},{258,2},{3,259},{259,3},{4... | collective-permute-start | bytes 3440648 | tf_op jit(solution)/shard_map/ppermute | solution.py:13
  667.1 2.5 collective-permute-done
  669.7 2.1 fusion.23
  (99 shorter events, 1.1 us)
Async XLA Ops:
  6.5 647.2 %copy-start = (bf16[128,5120]{1,0:T(8,128)(2,1)S(1)}, bf16[128,5120]{1,0:T(8,128)(2,1)}, u32[]{:S(2)}) copy-start(bf16[128,5120]{1,0:T(8,128)(2,1)} %param.18) | copy-start | bytes 3932164
  6.5 218.7 %all-gather.5.cloned.1.call-start = ((), (), s32[]{:S(2)}) async-start(), calls=%async_computation | async-start | bytes 7368704 | tf_op jit(solution)/shard_map/all_gather | solution.py:71
  7.3 434.4 %all-gather.7.cloned.1.call-start = ((), (), s32[]{:S(2)}) async-start(), calls=%async_computation.1 | async-start | bytes 7368704 | tf_op jit(solution)/shard_map/all_gather | solution.py:72
  441.6 212.1 %copy-start.3 = (f32[5120]{0:T(1024)S(1)}, f32[5120]{0:T(1024)}, u32[]{:S(2)}) copy-start(f32[5120]{0:T(1024)} %param.19) | copy-start | bytes 61444
  441.6 1.2 copy-start.1
  442.9 8.2 %copy-start.4 = (bf16[112,128]{1,0:T(8,128)(2,1)S(1)}, bf16[112,128]{1,0:T(8,128)(2,1)}, u32[]{:S(2)}) copy-start(bf16[112,128]{1,0:T(8,128)(2,1)} %get-tuple-element.308) | copy-start | bytes 86020 | tf_op jit(solution)/shard_map/while
  455.5 0.8 copy-start.2
  468.1 1.2 copy-start.1
  469.4 8.2 %copy-start.4 = (bf16[112,128]{1,0:T(8,128)(2,1)S(1)}, bf16[112,128]{1,0:T(8,128)(2,1)}, u32[]{:S(2)}) copy-start(bf16[112,128]{1,0:T(8,128)(2,1)} %get-tuple-element.308) | copy-start | bytes 86020 | tf_op jit(solution)/shard_map/while
  482.0 0.8 copy-start.2
  494.7 1.2 copy-start.1
  495.9 8.2 %copy-start.4 = (bf16[112,128]{1,0:T(8,128)(2,1)S(1)}, bf16[112,128]{1,0:T(8,128)(2,1)}, u32[]{:S(2)}) copy-start(bf16[112,128]{1,0:T(8,128)(2,1)} %get-tuple-element.308) | copy-start | bytes 86020 | tf_op jit(solution)/shard_map/while
  508.5 0.8 copy-start.2
  521.2 1.2 copy-start.1
  522.4 8.2 %copy-start.4 = (bf16[112,128]{1,0:T(8,128)(2,1)S(1)}, bf16[112,128]{1,0:T(8,128)(2,1)}, u32[]{:S(2)}) copy-start(bf16[112,128]{1,0:T(8,128)(2,1)} %get-tuple-element.308) | copy-start | bytes 86020 | tf_op jit(solution)/shard_map/while
  535.0 0.8 copy-start.2
  547.7 1.2 copy-start.1
  548.9 8.2 %copy-start.4 = (bf16[112,128]{1,0:T(8,128)(2,1)S(1)}, bf16[112,128]{1,0:T(8,128)(2,1)}, u32[]{:S(2)}) copy-start(bf16[112,128]{1,0:T(8,128)(2,1)} %get-tuple-element.308) | copy-start | bytes 86020 | tf_op jit(solution)/shard_map/while
  561.5 0.8 copy-start.2
  574.2 1.2 copy-start.1
  575.4 8.2 %copy-start.4 = (bf16[112,128]{1,0:T(8,128)(2,1)S(1)}, bf16[112,128]{1,0:T(8,128)(2,1)}, u32[]{:S(2)}) copy-start(bf16[112,128]{1,0:T(8,128)(2,1)} %get-tuple-element.308) | copy-start | bytes 86020 | tf_op jit(solution)/shard_map/while
  588.1 0.8 copy-start.2
  600.7 1.2 copy-start.1
  602.0 8.2 %copy-start.4 = (bf16[112,128]{1,0:T(8,128)(2,1)S(1)}, bf16[112,128]{1,0:T(8,128)(2,1)}, u32[]{:S(2)}) copy-start(bf16[112,128]{1,0:T(8,128)(2,1)} %get-tuple-element.308) | copy-start | bytes 86020 | tf_op jit(solution)/shard_map/while
  614.6 0.8 copy-start.2
  627.2 1.2 copy-start.1
  628.5 8.2 %copy-start.4 = (bf16[112,128]{1,0:T(8,128)(2,1)S(1)}, bf16[112,128]{1,0:T(8,128)(2,1)}, u32[]{:S(2)}) copy-start(bf16[112,128]{1,0:T(8,128)(2,1)} %get-tuple-element.308) | copy-start | bytes 86020 | tf_op jit(solution)/shard_map/while
  641.1 0.8 copy-start.2
  655.6 14.1 %collective-permute-start = (bf16[112,5120]{1,0:T(8,128)(2,1)S(1)}, bf16[112,5120]{1,0:T(8,128)(2,1)}, u32[]{:S(2)}, u32[]{:S(2)}) collective-permute-start(bf16[112,5120]{1,0:T(8,128)(2,1)S(1)} %fusion.21), channel_id=1, source_target_pairs={{0,256},{256,0},{1,257},{257,1},{2,258},{258,2},{3,259},{259,3},{4... | collective-permute-start | bytes 3440648 | tf_op jit(solution)/shard_map/ppermute | solution.py:13
Sparse Core Ops, SparseCore 0:
  11.7 213.5 all-gather.4
  229.6 211.9 all-gather.6
where the time goes:
time: 680 us; the launch traced here: 679 us
  waiting for transfers between devices  438 us (64%)
  local copies, waits for them, and re-layouts  138 us (20%)
  matrix products  67.4 us (10%)
  between operations  13.5 us (2%)
  starting transfers between devices  11.6 us (2%)
    all_gather x1, waiting for transfers between devices, on_device(): lax.all_gather(stale_keys[0], 'patch', axis=0, tiled=True)  217 us
    all_gather x1, waiting for transfers between devices, on_device(): lax.all_gather(stale_values[0], 'patch', axis=0, tiled=True)  216 us
    gather x8, local copies, waits for them, and re-layouts, refresh(): jnp.take(keys_fresh, offset, axis=0)  65.1 us
    gather x8, local copies, waits for them, and re-layouts, refresh(): jnp.take(values_fresh, offset, axis=0)  65 us
    dot_general x8, matrix products, attend_block(): lax.dot_general(query_rows, piece_keys, (((1,), (1,)), ((), ())), preferr...  35.6 us
    dot_general x8, matrix products, attend_block(): jnp.dot(weights, piece_values, preferred_element_type=jnp.float32)  30 us
  transfers between devices with their start and end apart: 3, of which 3 were waited for; matrix products, arithmetic and copies ran while one was open for 0% of the time, Pallas kernels for 0%

commit v1 on v0

--- a/solution.py
+++ b/solution.py
@@ -69,7 +69,10 @@
     )
     all_keys, all_values = (
         lax.all_gather(stale_keys[0], "patch", axis=0, tiled=True),
-        lax.all_gather(stale_values[0], "patch", axis=0, tiled=True),
+        jnp.concatenate(
+            lax.all_to_all(jnp.stack([stale_values[0]] * lax.axis_size("patch")), "patch", 0, 0),
+            axis=0,
+        ),
     )
     running = initial
     piece_keys = all_keys

time: 680 us -> 623 us (0.916)
  waiting for transfers between devices: 438 us -> 352 us
  starting transfers between devices: 11.6 us -> 32.7 us
    all_gather x1 -> x0, waiting for transfers between devices: 216 us -> none  [on_device(): lax.all_gather(stale_values[0], 'patch', axis=0, tiled=True)]
    all_gather x1, waiting for transfers between devices: 217 us -> 328 us  [on_device(): lax.all_gather(stale_keys[0], 'patch', axis=0, tiled=True)]
    all_to_all x0 -> x1, starting transfers between devices: none -> 26.4 us  [on_device(): lax.all_to_all(jnp.stack([stale_values[0]] * lax.axis_size('patch')), 'pa...]
    all_to_all x0 -> x1, waiting for transfers between devices: none -> 21.1 us  [on_device(): lax.all_to_all(jnp.stack([stale_values[0]] * lax.axis_size('patch')), 'pa...]
where the time goes in v1:
time: 623 us; the launch traced here: 617 us
  waiting for transfers between devices  352 us (57%)
  local copies, waits for them, and re-layouts  139 us (22%)
  matrix products  67.4 us (11%)
  starting transfers between devices  32.7 us (5%)
  between operations  13.5 us (2%)
    all_gather x1, waiting for transfers between devices, on_device(): lax.all_gather(stale_keys[0], 'patch', axis=0, tiled=True)  328 us
    gather x8, local copies, waits for them, and re-layouts, refresh(): jnp.take(values_fresh, offset, axis=0)  64.7 us
    gather x8, local copies, waits for them, and re-layouts, refresh(): jnp.take(keys_fresh, offset, axis=0)  64.7 us
    dot_general x8, matrix products, attend_block(): lax.dot_general(query_rows, piece_keys, (((1,), (1,)), ((), ())), preferr...  35.6 us
    dot_general x8, matrix products, attend_block(): jnp.dot(weights, piece_values, preferred_element_type=jnp.float32)  30 us
    all_to_all x1, starting transfers between devices, on_device(): lax.all_to_all(jnp.stack([stale_values[0]] * lax.axis_size('patch')), 'pa...  26.4 us
    all_to_all x1, waiting for transfers between devices, on_device(): lax.all_to_all(jnp.stack([stale_values[0]] * lax.axis_size('patch')), 'pa...  21.1 us
  transfers between devices with their start and end apart: 3, of which 3 were waited for; matrix products, arithmetic and copies ran while one was open for 0% of the time, Pallas kernels for 0%

profile of v1, /device:TPU:1, one launch (start us, length us, event | category | flops | bytes accessed | tf_op | source)
XLA Modules:
  0.0 616.8 jit_solution(14523078242265627327)
XLA Ops:
  6.5 0.0 copy-start
  6.5 4.7 stack.3
  11.3 26.4 %all-to-all-start = ((bf16[256,112,128]{2,1,0:T(8,128)(2,1)}), bf16[256,112,128]{2,1,0:T(8,128)(2,1)}, u32[]{:S(2)}, u32[]{:S(2)}) async-start(bf16[256,112,128]{2,1,0:T(8,128)(2,1)} %stack.3), calls=%async_computation | async-start | bytes 14680064 | tf_op jit(solution)/shard_map/all_to_all | solution.py:73
  37.7 0.0 all-gather.3.cloned.1.call-start
  37.7 0.7 all-gather.3.cloned.1.call-update
  38.4 327.7 %all-gather.3.cloned.1.call-done = bf16[1,28672,128]{2,1,0:T(8,128)(2,1)} async-done(((bf16[1,112,128]{2,1,0:T(8,128)(2,1)}), bf16[1,28672,128]{2,1,0:T(8,128)(2,1)}) %all-gather.3.cloned.1.call-update) | async-done | bytes 7340048 | tf_op jit(solution)/shard_map/all_gather | solution.py:71
  366.1 21.1 %all-to-all-done = bf16[256,112,128]{2,1,0:T(8,128)(2,1)} async-done(((bf16[256,112,128]{2,1,0:T(8,128)(2,1)}), bf16[256,112,128]{2,1,0:T(8,128)(2,1)}, u32[]{:S(2)}, u32[]{:S(2)}) %all-to-all-start) | async-done | bytes 7340064 | tf_op jit(solution)/shard_map/all_to_all | solution.py:73
  387.2 0.0 copy-done.1
  387.2 0.0 copy-done.2
  387.2 0.0 copy-done.4
  387.2 0.0 copy-start.3
  387.2 210.0 %while.16 = (s32[]{:T(128)}, f32[112]{0:T(128)S(1)}, f32[112]{0:T(128)S(1)}, f32[112,128]{1,0:T(8,128)S(1)}, s32[8]{0:T(128)S(1)}, /*index=5*/s32[]{:T(128)}, s3...) while((s32[]{:T(128)}, f32[112]{0:T(128)S(1)}, ...), condition=%wide.region_3.5_spmd.clone, body=%wide.region_0.4_spmd.clone.sunk | while | flops 210679344 | bytes 12403909 | solution.py:90
  387.2 0.7 dynamic_slice.46
  388.7 8.1 %gather_fusion = bf16[3584,128]{1,0:T(8,128)(2,1)} fusion(bf16[112,128]{1,0:T(8,128)(2,1)S(1)} %get-tuple-element.306, s32[4096]{0:T(1024)S(1)} %pad_clamp_fusion.2), kind=kCustom, calls=%fused_computation.clone.clone.1 | custom fusion | bytes 1849344 | tf_op jit(solution)/shard_map/while/body/eval_jaxpr/jit(_take)/gather | solution.py:41
  396.8 4.5 fusion.35
  401.2 0.4 convert_reduce_fusion.2
  401.6 8.1 %gather_fusion.1 = bf16[3584,128]{1,0:T(8,128)(2,1)} fusion(bf16[112,128]{1,0:T(8,128)(2,1)S(1)} %get-tuple-element.309, s32[4096]{0:T(1024)S(1)} %pad_clamp_fusion.2), kind=kCustom, calls=%fused_computation.1.clone.clone.1 | custom fusion | bytes 1849344 | tf_op jit(solution)/shard_map/while/body/eval_jaxpr/jit(_take)/gather | solution.py:43
  409.7 3.8 convolution_add_fusion.2
  413.5 0.7 dynamic_slice.46
  414.9 8.1 %gather_fusion = bf16[3584,128]{1,0:T(8,128)(2,1)} fusion(bf16[112,128]{1,0:T(8,128)(2,1)S(1)} %get-tuple-element.306, s32[4096]{0:T(1024)S(1)} %pad_clamp_fusion.2), kind=kCustom, calls=%fused_computation.clone.clone.1 | custom fusion | bytes 1849344 | tf_op jit(solution)/shard_map/while/body/eval_jaxpr/jit(_take)/gather | solution.py:41
  423.0 4.4 fusion.35
  427.5 0.4 convert_reduce_fusion.2
  427.9 8.1 %gather_fusion.1 = bf16[3584,128]{1,0:T(8,128)(2,1)} fusion(bf16[112,128]{1,0:T(8,128)(2,1)S(1)} %get-tuple-element.309, s32[4096]{0:T(1024)S(1)} %pad_clamp_fusion.2), kind=kCustom, calls=%fused_computation.1.clone.clone.1 | custom fusion | bytes 1849344 | tf_op jit(solution)/shard_map/while/body/eval_jaxpr/jit(_take)/gather | solution.py:43
  436.0 3.8 convolution_add_fusion.2
  439.7 0.7 dynamic_slice.46
  441.2 8.1 %gather_fusion = bf16[3584,128]{1,0:T(8,128)(2,1)} fusion(bf16[112,128]{1,0:T(8,128)(2,1)S(1)} %get-tuple-element.306, s32[4096]{0:T(1024)S(1)} %pad_clamp_fusion.2), kind=kCustom, calls=%fused_computation.clone.clone.1 | custom fusion | bytes 1849344 | tf_op jit(solution)/shard_map/while/body/eval_jaxpr/jit(_take)/gather | solution.py:41
  449.3 4.5 fusion.35
  453.7 0.4 convert_reduce_fusion.2
  454.1 8.1 %gather_fusion.1 = bf16[3584,128]{1,0:T(8,128)(2,1)} fusion(bf16[112,128]{1,0:T(8,128)(2,1)S(1)} %get-tuple-element.309, s32[4096]{0:T(1024)S(1)} %pad_clamp_fusion.2), kind=kCustom, calls=%fused_computation.1.clone.clone.1 | custom fusion | bytes 1849344 | tf_op jit(solution)/shard_map/while/body/eval_jaxpr/jit(_take)/gather | solution.py:43
  462.2 3.8 convolution_add_fusion.2
  466.0 0.7 dynamic_slice.46
  467.4 8.1 %gather_fusion = bf16[3584,128]{1,0:T(8,128)(2,1)} fusion(bf16[112,128]{1,0:T(8,128)(2,1)S(1)} %get-tuple-element.306, s32[4096]{0:T(1024)S(1)} %pad_clamp_fusion.2), kind=kCustom, calls=%fused_computation.clone.clone.1 | custom fusion | bytes 1849344 | tf_op jit(solution)/shard_map/while/body/eval_jaxpr/jit(_take)/gather | solution.py:41
  475.5 4.4 fusion.35
  480.0 0.4 convert_reduce_fusion.2
  480.4 8.1 %gather_fusion.1 = bf16[3584,128]{1,0:T(8,128)(2,1)} fusion(bf16[112,128]{1,0:T(8,128)(2,1)S(1)} %get-tuple-element.309, s32[4096]{0:T(1024)S(1)} %pad_clamp_fusion.2), kind=kCustom, calls=%fused_computation.1.clone.clone.1 | custom fusion | bytes 1849344 | tf_op jit(solution)/shard_map/while/body/eval_jaxpr/jit(_take)/gather | solution.py:43
  488.5 3.8 convolution_add_fusion.2
  492.2 0.7 dynamic_slice.46
  493.7 8.1 %gather_fusion = bf16[3584,128]{1,0:T(8,128)(2,1)} fusion(bf16[112,128]{1,0:T(8,128)(2,1)S(1)} %get-tuple-element.306, s32[4096]{0:T(1024)S(1)} %pad_clamp_fusion.2), kind=kCustom, calls=%fused_computation.clone.clone.1 | custom fusion | bytes 1849344 | tf_op jit(solution)/shard_map/while/body/eval_jaxpr/jit(_take)/gather | solution.py:41
  501.8 4.5 fusion.35
  506.2 0.4 convert_reduce_fusion.2
  506.6 8.1 %gather_fusion.1 = bf16[3584,128]{1,0:T(8,128)(2,1)} fusion(bf16[112,128]{1,0:T(8,128)(2,1)S(1)} %get-tuple-element.309, s32[4096]{0:T(1024)S(1)} %pad_clamp_fusion.2), kind=kCustom, calls=%fused_computation.1.clone.clone.1 | custom fusion | bytes 1849344 | tf_op jit(solution)/shard_map/while/body/eval_jaxpr/jit(_take)/gather | solution.py:43
  514.7 3.8 convolution_add_fusion.2
  518.5 0.7 dynamic_slice.46
  519.9 8.1 %gather_fusion = bf16[3584,128]{1,0:T(8,128)(2,1)} fusion(bf16[112,128]{1,0:T(8,128)(2,1)S(1)} %get-tuple-element.306, s32[4096]{0:T(1024)S(1)} %pad_clamp_fusion.2), kind=kCustom, calls=%fused_computation.clone.clone.1 | custom fusion | bytes 1849344 | tf_op jit(solution)/shard_map/while/body/eval_jaxpr/jit(_take)/gather | solution.py:41
  528.0 4.4 fusion.35
  532.5 0.4 convert_reduce_fusion.2
  532.9 8.1 %gather_fusion.1 = bf16[3584,128]{1,0:T(8,128)(2,1)} fusion(bf16[112,128]{1,0:T(8,128)(2,1)S(1)} %get-tuple-element.309, s32[4096]{0:T(1024)S(1)} %pad_clamp_fusion.2), kind=kCustom, calls=%fused_computation.1.clone.clone.1 | custom fusion | bytes 1849344 | tf_op jit(solution)/shard_map/while/body/eval_jaxpr/jit(_take)/gather | solution.py:43
  541.0 3.8 convolution_add_fusion.2
  544.8 0.7 dynamic_slice.46
  546.2 8.1 %gather_fusion = bf16[3584,128]{1,0:T(8,128)(2,1)} fusion(bf16[112,128]{1,0:T(8,128)(2,1)S(1)} %get-tuple-element.306, s32[4096]{0:T(1024)S(1)} %pad_clamp_fusion.2), kind=kCustom, calls=%fused_computation.clone.clone.1 | custom fusion | bytes 1849344 | tf_op jit(solution)/shard_map/while/body/eval_jaxpr/jit(_take)/gather | solution.py:41
  554.3 4.5 fusion.35
  558.7 0.4 convert_reduce_fusion.2
  559.1 8.1 %gather_fusion.1 = bf16[3584,128]{1,0:T(8,128)(2,1)} fusion(bf16[112,128]{1,0:T(8,128)(2,1)S(1)} %get-tuple-element.309, s32[4096]{0:T(1024)S(1)} %pad_clamp_fusion.2), kind=kCustom, calls=%fused_computation.1.clone.clone.1 | custom fusion | bytes 1849344 | tf_op jit(solution)/shard_map/while/body/eval_jaxpr/jit(_take)/gather | solution.py:43
  567.2 3.8 convolution_add_fusion.2
  571.0 0.7 dynamic_slice.46
  572.4 8.1 %gather_fusion = bf16[3584,128]{1,0:T(8,128)(2,1)} fusion(bf16[112,128]{1,0:T(8,128)(2,1)S(1)} %get-tuple-element.306, s32[4096]{0:T(1024)S(1)} %pad_clamp_fusion.2), kind=kCustom, calls=%fused_computation.clone.clone.1 | custom fusion | bytes 1849344 | tf_op jit(solution)/shard_map/while/body/eval_jaxpr/jit(_take)/gather | solution.py:41
  580.5 4.4 fusion.35
  585.0 0.4 convert_reduce_fusion.2
  585.4 8.1 %gather_fusion.1 = bf16[3584,128]{1,0:T(8,128)(2,1)} fusion(bf16[112,128]{1,0:T(8,128)(2,1)S(1)} %get-tuple-element.309, s32[4096]{0:T(1024)S(1)} %pad_clamp_fusion.2), kind=kCustom, calls=%fused_computation.1.clone.clone.1 | custom fusion | bytes 1849344 | tf_op jit(solution)/shard_map/while/body/eval_jaxpr/jit(_take)/gather | solution.py:43
  593.5 3.8 convolution_add_fusion.2
  597.3 1.8 fusion.21
  599.1 6.2 %collective-permute-start = (bf16[112,5120]{1,0:T(8,128)(2,1)S(1)}, bf16[112,5120]{1,0:T(8,128)(2,1)}, u32[]{:S(2)}, u32[]{:S(2)}) collective-permute-start(bf16[112,5120]{1,0:T(8,128)(2,1)S(1)} %fusion.21), channel_id=1, source_target_pairs={{0,256},{256,0},{1,257},{257,1},{2,258},{258,2},{3,259},{259,3},{4... | collective-permute-start | bytes 3440648 | tf_op jit(solution)/shard_map/ppermute | solution.py:13
  605.3 2.5 collective-permute-done
  607.8 2.2 fusion.23
  (57 shorter events, 0.6 us)
Async XLA Ops:
  6.5 590.7 %copy-start = (bf16[128,5120]{1,0:T(8,128)(2,1)S(1)}, bf16[128,5120]{1,0:T(8,128)(2,1)}, u32[]{:S(2)}) copy-start(bf16[128,5120]{1,0:T(8,128)(2,1)} %param.18) | copy-start | bytes 3932164
  11.3 376.0 %copy-start.1 = (bf16[1,112,128]{2,1,0:T(8,128)(2,1)S(1)}, bf16[1,112,128]{2,1,0:T(8,128)(2,1)}, u32[]{:S(2)}) copy-start(bf16[1,112,128]{2,1,0:T(8,128)(2,1)} %param.13) | copy-start | bytes 86020
  11.3 376.0 %copy-start.2 = (bf16[1,112,128]{2,1,0:T(8,128)(2,1)S(1)}, bf16[1,112,128]{2,1,0:T(8,128)(2,1)}, u32[]{:S(2)}) copy-start(bf16[1,112,128]{2,1,0:T(8,128)(2,1)} %param.14) | copy-start | bytes 86020
  11.3 376.0 %copy-start.4 = (bf16[1,112,128]{2,1,0:T(8,128)(2,1)S(1)}, bf16[1,112,128]{2,1,0:T(8,128)(2,1)}, u32[]{:S(2)}) copy-start(bf16[1,112,128]{2,1,0:T(8,128)(2,1)} %param.12) | copy-start | bytes 86020
  11.3 375.9 %all-to-all-start = ((bf16[256,112,128]{2,1,0:T(8,128)(2,1)}), bf16[256,112,128]{2,1,0:T(8,128)(2,1)}, u32[]{:S(2)}, u32[]{:S(2)}) async-start(bf16[256,112,128]{2,1,0:T(8,128)(2,1)} %stack.3), calls=%async_computation | async-start | bytes 14680064 | tf_op jit(solution)/shard_map/all_to_all | solution.py:73
  37.7 328.5 %all-gather.3.cloned.1.call-start = ((), (), s32[]{:S(2)}) async-start(), calls=%async_computation.1 | async-start | bytes 7368704 | tf_op jit(solution)/shard_map/all_gather | solution.py:71
  387.2 210.0 %copy-start.3 = (f32[5120]{0:T(1024)S(1)}, f32[5120]{0:T(1024)}, u32[]{:S(2)}) copy-start(f32[5120]{0:T(1024)} %param.19) | copy-start | bytes 61444
  599.1 8.8 %collective-permute-start = (bf16[112,5120]{1,0:T(8,128)(2,1)S(1)}, bf16[112,5120]{1,0:T(8,128)(2,1)}, u32[]{:S(2)}, u32[]{:S(2)}) collective-permute-start(bf16[112,5120]{1,0:T(8,128)(2,1)S(1)} %fusion.21), channel_id=1, source_target_pairs={{0,256},{256,0},{1,257},{257,1},{2,258},{258,2},{3,259},{259,3},{4... | collective-permute-start | bytes 3440648 | tf_op jit(solution)/shard_map/ppermute | solution.py:13
Sparse Core Ops, SparseCore 0:
  42.8 323.2 all-gather.2
